TPU v7x, 512 devices: a whole 4x8x8 slice. The times are simulated.
512 devices in a mesh: expert: 32 (over y, x), tensor: 16 (over z, core).
Axes of the slice: x: 4, y: 8, z: 8, core: 2. Of those that a mesh axis runs over, the one named last changes fastest.
Arguments:
- residual: bfloat16 [2048, 7168], P('expert', 'tensor'), may hold values from -40 to 40
- attn_parts: bfloat16 [16, 2048, 7168], P('tensor', 'expert'), may hold values from -2 to 2
- norm_gain: bfloat16 [7168], P('tensor'), may hold values from 0.099609375 to 1.8984375
- routes: int32 [2048, 8], P('expert'), may hold values from 0 to 31, all different within a row; in each aligned block of 64 rows (0 to 63, 64 to 127, ...) at most 24 rows name the same one
- route_weights: float32 [2048, 8], P('expert'), may hold values from 0.05 to 0.6
- w_gate: bfloat16 [32, 7168, 2048], P('expert', None, 'tensor'), may hold values from -0.06023809 to 0.06023809
- w_gate_q: bfloat16 [32, 7168, 2048], P('expert', None, 'tensor'), may hold values from -0.09567226 to 0.09567226
Outputs:
- token_error: float32 [2048], P('expert')
- expert_error: float32 [32], P('expert')
- hess_diag: float32 [32, 7168], P('expert', 'tensor')
Inputs may be any that keep to these rules, and one draw needn't show every extreme that they name: `routes`: no expert is named by more than 24 of the rows of one device, and in every draw some expert is named by exactly 24 of them; the 8 experts of a token are distinct; every expert is named by some token.
All inputs are finite; a program needn't handle non-finite values.
Results may differ from a plain program's by a relative error of at most 0.0023.
Values may be sent and summed in bfloat16 or wider, within the bound.
A program may use at most 64 MiB of HBM per device.

v0:
```python
import jax
import jax.numpy as jnp
from jax import lax
from jax.sharding import PartitionSpec as P

D = 7168
FF = 2048
CAP = 24
epsilon = 1e-06


def per_device(residual, attn_parts, norm_gain, routes, route_weights, w_gate, w_gate_q):
    n_expert = lax.axis_size("expert")
    tok_count = residual.shape[0]
    local_cols = residual.shape[1]
    top_count = routes.shape[1]
    gain_wide = norm_gain.astype(jnp.float32)[None, :]
    summed = lax.psum_scatter(
        attn_parts[0].astype(jnp.float32).astype(jnp.bfloat16),
        "tensor",
        scatter_dimension=1,
        tiled=True,
    ).astype(jnp.float32)
    hidden = residual.astype(jnp.float32) + summed
    squares = lax.psum(jnp.sum(hidden * hidden, axis=1), "tensor")
    scaling = lax.rsqrt(squares / D + epsilon)
    normed = (hidden * scaling[:, None] * gain_wide).astype(jnp.bfloat16)
    expert_ids = jnp.arange(n_expert, dtype=jnp.int32)
    flat_routes = routes.reshape(-1)
    one_hot = (flat_routes[:, None] == expert_ids[None, :]).astype(jnp.int32)
    earlier = jnp.cumsum(one_hot, axis=0) - one_hot
    slot_index = jnp.sum(earlier * one_hot, axis=1)
    target = flat_routes * CAP + slot_index
    load_counts = jnp.sum(one_hot, axis=0)
    slot_ids = jnp.arange(n_expert * CAP, dtype=jnp.int32)
    placing = (slot_ids[:, None] == target[None, :]).reshape(n_expert * CAP, tok_count, top_count)
    dispatch = jnp.sum(placing.astype(jnp.int32), axis=2).astype(jnp.bfloat16)
    count_send = load_counts.astype(jnp.bfloat16).reshape(n_expert, 1)
    weight_full = w_gate[0]
    weight_quant = w_gate_q[0]
    outgoing = jnp.dot(dispatch, normed, preferred_element_type=jnp.float32).astype(jnp.bfloat16)
    outgoing = outgoing.reshape(n_expert, CAP, local_cols)
    arrived, arrived_counts = (
        lax.all_to_all(outgoing, "expert", split_axis=0, concat_axis=0, tiled=True),
        lax.all_to_all(count_send, "expert", split_axis=0, concat_axis=0, tiled=True),
    )
    own_block = arrived.reshape(n_expert * CAP, local_cols)
    column_block = lax.all_gather(own_block, "tensor", axis=1, tiled=True)
    full_acc = jnp.dot(column_block, weight_full, preferred_element_type=jnp.float32)
    quant_acc = jnp.dot(column_block, weight_quant, preferred_element_type=jnp.float32)
    block_squares = jnp.einsum("rc,rc->c", own_block, own_block, preferred_element_type=jnp.float32)
    total_load = jnp.sum(arrived_counts.astype(jnp.float32))
    hess_local = 2.0 * block_squares / total_load
    difference = full_acc - quant_acc
    err_part = (jnp.sum(difference * difference, axis=1) / FF).reshape(n_expert, CAP)
    pow_part = (jnp.sum(full_acc * full_acc, axis=1) / FF).reshape(n_expert, CAP)
    err_slots, pow_slots = lax.psum((err_part, pow_part), "tensor")
    expert_total = jnp.sum(err_slots) / (jnp.sum(pow_slots) + epsilon)
    back_err, back_pow = (
        lax.all_to_all(err_slots, "expert", split_axis=0, concat_axis=0, tiled=True),
        lax.all_to_all(pow_slots, "expert", split_axis=0, concat_axis=0, tiled=True),
    )
    token_err = jnp.take(back_err.reshape(-1), target).reshape(tok_count, top_count)
    token_pow = jnp.take(back_pow.reshape(-1), target).reshape(tok_count, top_count)
    ratios = token_err / (token_pow + epsilon)
    token_error = jnp.sum(route_weights * ratios, axis=1)
    return (token_error, expert_total.reshape(1), hess_local.reshape(1, local_cols))


def solution(mesh):
    placed = (
        P("expert", "tensor"),
        P("tensor", "expert", None),
        P("tensor"),
        P("expert", None),
        P("expert", None),
        P("expert", None, "tensor"),
        P("expert", None, "tensor"),
    )
    return jax.shard_map(
        per_device,
        mesh=mesh,
        in_specs=placed,
        out_specs=(P("expert"), P("expert"), P("expert", "tensor")),
        check_vma=False,
    )
```

profile of v0, /device:TPU:2, one launch (start us, length us, event | category | flops | bytes accessed | tf_op | source)
XLA Modules:
  0.0 304.8 jit_solution(2115498877063809150)
XLA Ops:
  7.2 2.7 copy.57
  10.4 1.2 reduce-window.6
  12.8 65.0 %reduce-scatter.4.cloned.1.call-done = bf16[448,64]{1,0:T(8,128)(2,1)} async-done(((bf16[7168,64]{1,0:T(8,128)(2,1)}), bf16[448,64]{1,0:T(8,128)(2,1)}) %reduce-scatter.4.cloned.1.call-update) | async-done | bytes 57360
  77.8 1.0 copy.58
  78.9 23.6 %psum.21 = f32[64]{0:T(128)S(1)} all-reduce(f32[64]{0:T(128)S(1)} %multiply_reduce_fusion.1), channel_id=1, replica_groups=mesh['expert'=32,'tensor'=16] {'tensor'}, use_global_device_ids=true, to_apply=%region_6.7 | all-reduce | flops 64 | bytes 512 | tf_op jit(solution)/shard_map/psum | solution.py:25
  103.3 32.0 %all_to_all.29 = bf16[32,24,448]{2,1,0:T(8,128)(2,1)S(1)} all-to-all(bf16[32,24,448]{2,1,0:T(8,128)(2,1)S(1)} %bitcast.49), channel_id=1, replica_groups=mesh['expert'=32,'tensor'=16] {'expert'}, dimensions={0} | all-to-all | bytes 1376256 | tf_op jit(solution)/shard_map/all_to_all | solution.py:44
  135.4 1.1 copy.46
  136.5 0.7 copy.50
  137.2 5.6 %all-to-all-start.3 = ((bf16[32,1,1]{2,1,0:T(2,128)(2,1)}), bf16[32,1,1]{2,1,0:T(2,128)(2,1)S(1)}, u32[]{:S(2)}, u32[]{:S(2)}) async-start(bf16[32,1,1]{2,1,0:T(2,128)(2,1)} %copy.50), calls=%async_computation.3 | async-start | bytes 32768 | tf_op jit(solution)/shard_map/all_to_all | solution.py:45
  142.9 8.4 %all-to-all-done.3 = bf16[32,1,1]{2,1,0:T(2,128)(2,1)S(1)} async-done(((bf16[32,1,1]{2,1,0:T(2,128)(2,1)}), bf16[32,1,1]{2,1,0:T(2,128)(2,1)S(1)}, u32[]{:S(2)}, u32[]{:S(2)}) %all-to-all-start.3) | async-done | bytes 96 | tf_op jit(solution)/shard_map/all_to_all | solution.py:45
  152.0 49.7 %all-gather.2.cloned.1.call-done = bf16[768,7168]{0,1:T(8,128)(2,1)} async-done(((bf16[768,448]{0,1:T(8,128)(2,1)}), bf16[768,7168]{0,1:T(8,128)(2,1)}) %all-gather.2.cloned.1.call-update) | async-done | bytes 11010064 | tf_op jit(solution)/shard_map/all_gather | solution.py:48
  201.7 6.0 %multiply_reduce_fusion = (f32[768]{0:T(1024)S(1)}, f32[768,128]{0,1:T(8,128)S(1)}) fusion(bf16[768,7168]{0,1:T(8,128)(2,1)} %all-gather.2.cloned.1.call-done, bf16[1,7168,128]{2,1,0:T(8,128)(2,1)S(1)} %copy-done), kind=kOutput, calls=%fused_computation.14 | convolution fusion | flops 1409481984 | bytes 13241344 | tf_op jit(solution)/shard_map/dot_general | solution.py:49
  207.7 1.2 copy-done.5
  209.4 1.8 fusion.11
  211.4 47.3 %all-reduce = (f32[32,24]{1,0:T(8,128)}, f32[32,24]{1,0:T(8,128)}) all-reduce(f32[32,24]{1,0:T(8,128)S(1)} %div.36, f32[32,24]{1,0:T(8,128)S(1)} %div.34), channel_id=1, replica_groups=mesh['expert'=32,'tensor'=16] {'tensor'}, use_global_device_ids=true, to_apply=%region_10.12 | all-reduce | flops 1536 | bytes 12288 | tf_op jit(solution)/shard_map/psum | solution.py:57
  258.7 9.9 %all-to-all-start.1 = ((f32[32,1,24]{2,1,0:T(1,128)}), f32[32,1,24]{2,1,0:T(1,128)S(1)}, u32[]{:S(2)}, u32[]{:S(2)}) async-start(f32[32,1,24]{2,1,0:T(1,128)} %bitcast.9), calls=%async_computation.1 | async-start | bytes 32768 | tf_op jit(solution)/shard_map/all_to_all | solution.py:60
  268.9 8.3 %all-to-all-done.1 = f32[32,1,24]{2,1,0:T(1,128)S(1)} async-done(((f32[32,1,24]{2,1,0:T(1,128)}), f32[32,1,24]{2,1,0:T(1,128)S(1)}, u32[]{:S(2)}, u32[]{:S(2)}) %all-to-all-start.1) | async-done | bytes 3104 | tf_op jit(solution)/shard_map/all_to_all | solution.py:60
  277.1 5.0 %all-to-all-start.2 = ((f32[32,1,24]{2,1,0:T(1,128)}), f32[32,1,24]{2,1,0:T(1,128)S(1)}, u32[]{:S(2)}, u32[]{:S(2)}) async-start(f32[32,1,24]{2,1,0:T(1,128)} %bitcast.11), calls=%async_computation.2 | async-start | bytes 32768 | tf_op jit(solution)/shard_map/all_to_all | solution.py:61
  282.1 1.2 multiply_divide_fusion
  283.3 1.3 reduce_sum.99
  284.7 1.3 reduce_sum.100
  288.6 2.1 all-to-all-done.2
  291.5 2.3 gather_fusion
  293.8 2.3 gather_fusion.1
  (53 shorter events, 6.9 us)
Async XLA Ops:
  7.2 194.5 %copy-start = (bf16[1,7168,128]{2,1,0:T(8,128)(2,1)S(1)}, bf16[1,7168,128]{2,1,0:T(8,128)(2,1)}, u32[]{:S(2)}) copy-start(bf16[1,7168,128]{2,1,0:T(8,128)(2,1)} %param.14) | copy-start | bytes 5505028
  7.2 70.6 %reduce-scatter.4.cloned.1.call-start = ((), (), s32[]{:S(2)}) async-start(), calls=%async_computation.6 | async-start | bytes 1949696
  7.2 2.8 copy-start.2
  7.2 3.1 %copy-start.4 = (bf16[448]{0:T(512)(128)(2,1)S(1)}, bf16[448]{0:T(512)(128)(2,1)}, u32[]{:S(2)}) copy-start(bf16[448]{0:T(512)(128)(2,1)} %param.11) | copy-start | bytes 2692
  10.0 68.8 %copy-start.1 = (bf16[64,448]{1,0:T(8,128)(2,1)S(1)}, bf16[64,448]{1,0:T(8,128)(2,1)}, u32[]{:S(2)}) copy-start(bf16[64,448]{1,0:T(8,128)(2,1)} %param.9) | copy-start | bytes 172036
  10.0 191.6 %all-gather.2.cloned.1.call-start = ((), (), s32[]{:S(2)}) async-start(), calls=%async_computation.5 | async-start | bytes 11698176 | tf_op jit(solution)/shard_map/all_gather | solution.py:48
  103.3 39.5 %copy-start.3 = (f32[64,8]{0,1:T(8,128)S(1)}, f32[64,8]{0,1:T(8,128)}, u32[]{:S(2)}) copy-start(f32[64,8]{0,1:T(8,128)} %param.13) | copy-start | bytes 6148
  137.2 14.1 %all-to-all-start.3 = ((bf16[32,1,1]{2,1,0:T(2,128)(2,1)}), bf16[32,1,1]{2,1,0:T(2,128)(2,1)S(1)}, u32[]{:S(2)}, u32[]{:S(2)}) async-start(bf16[32,1,1]{2,1,0:T(2,128)(2,1)} %copy.50), calls=%async_computation.3 | async-start | bytes 32768 | tf_op jit(solution)/shard_map/all_to_all | solution.py:45
  201.7 7.3 %copy-start.5 = (bf16[768,7168]{0,1:T(8,128)(2,1)S(1)}, bf16[768,7168]{0,1:T(8,128)(2,1)}, u32[]{:S(2)}) copy-start(bf16[768,7168]{0,1:T(8,128)(2,1)} %all-gather.2.cloned.1.call-done) | copy-start | bytes 33030148
  201.7 7.8 %copy-start.6 = (bf16[1,7168,128]{2,1,0:T(8,128)(2,1)S(1)}, bf16[1,7168,128]{2,1,0:T(8,128)(2,1)}, u32[]{:S(2)}) copy-start(bf16[1,7168,128]{2,1,0:T(8,128)(2,1)} %param.15) | copy-start | bytes 5505028
  258.7 18.4 %all-to-all-start.1 = ((f32[32,1,24]{2,1,0:T(1,128)}), f32[32,1,24]{2,1,0:T(1,128)S(1)}, u32[]{:S(2)}, u32[]{:S(2)}) async-start(f32[32,1,24]{2,1,0:T(1,128)} %bitcast.9), calls=%async_computation.1 | async-start | bytes 32768 | tf_op jit(solution)/shard_map/all_to_all | solution.py:60
  277.1 13.6 %all-to-all-start.2 = ((f32[32,1,24]{2,1,0:T(1,128)}), f32[32,1,24]{2,1,0:T(1,128)S(1)}, u32[]{:S(2)}, u32[]{:S(2)}) async-start(f32[32,1,24]{2,1,0:T(1,128)} %bitcast.11), calls=%async_computation.2 | async-start | bytes 32768 | tf_op jit(solution)/shard_map/all_to_all | solution.py:61
Sparse Core Ops, SparseCore 0:
  10.9 66.9 reduce-scatter.3
  136.6 64.9 all-gather.1
where the time goes:
time: 305 us
  waiting for transfers between devices  134 us (44%)
  blocking collectives  103 us (34%)
  starting transfers between devices  20.5 us (7%)
  between operations  16.7 us (5%)
  local copies, waits for them, and re-layouts  13.9 us (5%)
  other arithmetic  8.86 us (3%)
  matrix products  8.29 us (3%)
    unnamed x3, waiting for transfers between devices  65.1 us
    all_gather x1, waiting for transfers between devices, per_device(): column_block = lax.all_gather(own_block, 'tensor', axis=1, tiled=True)  49.7 us
    psum x1, blocking collectives, per_device(): err_slots, pow_slots = lax.psum((err_part, pow_part), 'tensor')  47.3 us
    all_to_all x1, blocking collectives, per_device(): lax.all_to_all(outgoing, 'expert', split_axis=0, concat_axis=0, tiled=True)  32 us
    psum x1, blocking collectives, per_device(): squares = lax.psum(jnp.sum(hidden * hidden, axis=1), 'tensor')  23.6 us
    all_to_all x1, starting transfers between devices, per_device(): lax.all_to_all(err_slots, 'expert', split_axis=0, concat_axis=0, tiled=True)  9.87 us
    all_to_all x1, waiting for transfers between devices, per_device(): lax.all_to_all(count_send, 'expert', split_axis=0, concat_axis=0, tiled=T...  8.4 us
    all_to_all x1, waiting for transfers between devices, per_device(): lax.all_to_all(err_slots, 'expert', split_axis=0, concat_axis=0, tiled=True)  8.25 us
  transfers between devices with their start and end apart: 5, of which 5 were waited for; matrix products, arithmetic and copies ran while one was open for 3% of the time, Pallas kernels for 0%

commit v1 on v0

--- a/solution.py
+++ b/solution.py
@@ -45,7 +45,9 @@
         lax.all_to_all(count_send, "expert", split_axis=0, concat_axis=0, tiled=True),
     )
     own_block = arrived.reshape(n_expert * CAP, local_cols)
-    column_block = lax.all_gather(own_block, "tensor", axis=1, tiled=True)
+    column_block = jnp.concatenate(
+        lax.all_to_all(jnp.stack([own_block] * lax.axis_size("tensor")), "tensor", 0, 0), axis=1
+    )
     full_acc = jnp.dot(column_block, weight_full, preferred_element_type=jnp.float32)
     quant_acc = jnp.dot(column_block, weight_quant, preferred_element_type=jnp.float32)
     block_squares = jnp.einsum("rc,rc->c", own_block, own_block, preferred_element_type=jnp.float32)

time: 305 us -> 502 us (1.65)
  waiting for transfers between devices: 134 us -> 345 us
  blocking collectives: 103 us -> 70.6 us
  starting transfers between devices: 20.5 us -> 30.1 us
    all_to_all x0 -> x2, waiting for transfers between devices: none -> 261 us  [the longest x1 240 us: per_device(): lax.all_to_all(jnp.stack([own_block] * lax.axis_size('tensor')), 'tensor'...]
    all_gather x1 -> x0, waiting for transfers between devices: 49.7 us -> none  [per_device(): column_block = lax.all_gather(own_block, 'tensor', axis=1, tiled=True)]
    all_to_all x1 -> x0, blocking collectives: 32 us -> none  [per_device(): lax.all_to_all(outgoing, 'expert', split_axis=0, concat_axis=0, tiled=True)]
    all_to_all x0 -> x2, starting transfers between devices: none -> 14.9 us  [the longest x1 9.88 us: per_device(): lax.all_to_all(outgoing, 'expert', split_axis=0, concat_axis=0, tiled=True)]
    another operation x1 -> x3, local copies, waits for them, and re-layouts: 0.01 us -> 5.36 us  [the longest x2 5.36 us: per_device(): jnp.stack([own_block] * lax.axis_size('tensor'))]
    all_to_all x1, starting transfers between devices: 9.87 us -> 4.71 us  [per_device(): lax.all_to_all(err_slots, 'expert', split_axis=0, concat_axis=0, tiled=True)]
    unnamed x3 -> x2, waiting for transfers between devices: 65.1 us -> 65.1 us
  transfers between devices with their start and end apart: 5 -> 6, of which waited for: 5 -> 6; matrix products, arithmetic and copies ran while one was open for 3% -> 2% of each run, Pallas kernels for 0% -> 0%
where the time goes in v1:
time: 502 us; the launch traced here: 501 us
  waiting for transfers between devices  345 us (69%)
  blocking collectives  70.6 us (14%)
  starting transfers between devices  30.1 us (6%)
  local copies, waits for them, and re-layouts  17.3 us (3%)
  between operations  16.7 us (3%)
  matrix products  12.4 us (2%)
  other arithmetic  8.87 us (2%)
    all_to_all x1, waiting for transfers between devices, per_device(): lax.all_to_all(jnp.stack([own_block] * lax.axis_size('tensor')), 'tensor'...  240 us
    unnamed x2, waiting for transfers between devices  65.1 us
    psum x1, blocking collectives, per_device(): err_slots, pow_slots = lax.psum((err_part, pow_part), 'tensor')  46.9 us
    psum x1, blocking collectives, per_device(): squares = lax.psum(jnp.sum(hidden * hidden, axis=1), 'tensor')  23.6 us
    all_to_all x1, waiting for transfers between devices, per_device(): lax.all_to_all(outgoing, 'expert', split_axis=0, concat_axis=0, tiled=True)  21.7 us
  transfers between devices with their start and end apart: 6, of which 6 were waited for; matrix products, arithmetic and copies ran while one was open for 2% of the time, Pallas kernels for 0%

profile of v1, /device:TPU:2, one launch (start us, length us, event | category | flops | bytes accessed | tf_op | source)
XLA Modules:
  0.0 501.1 jit_solution(15632526722423548934)
XLA Ops:
  7.2 2.7 copy.59
  10.3 1.2 reduce-window.6
  12.7 65.0 %reduce-scatter.4.cloned.1.call-done = bf16[448,64]{1,0:T(8,128)(2,1)} async-done(((bf16[7168,64]{1,0:T(8,128)(2,1)}), bf16[448,64]{1,0:T(8,128)(2,1)}) %reduce-scatter.4.cloned.1.call-update) | async-done | bytes 57360
  78.9 23.6 %psum.21 = f32[64]{0:T(128)S(1)} all-reduce(f32[64]{0:T(128)S(1)} %multiply_reduce_fusion.1), channel_id=1, replica_groups=mesh['expert'=32,'tensor'=16] {'tensor'}, use_global_device_ids=true, to_apply=%region_6.7 | all-reduce | flops 64 | bytes 512 | tf_op jit(solution)/shard_map/psum | solution.py:25
  103.0 1.2 copy.47
  104.2 9.9 %all-to-all-start = ((bf16[32,24,448]{2,1,0:T(8,128)(2,1)}), bf16[32,24,448]{2,1,0:T(8,128)(2,1)S(1)}, u32[]{:S(2)}, u32[]{:S(2)}) async-start(bf16[32,24,448]{2,1,0:T(8,128)(2,1)} %bitcast.4), calls=%async_computation | async-start | bytes 1572864 | tf_op jit(solution)/shard_map/all_to_all | solution.py:44
  114.8 21.7 %all-to-all-done = bf16[32,24,448]{2,1,0:T(8,128)(2,1)S(1)} async-done(((bf16[32,24,448]{2,1,0:T(8,128)(2,1)}), bf16[32,24,448]{2,1,0:T(8,128)(2,1)S(1)}, u32[]{:S(2)}, u32[]{:S(2)}) %all-to-all-start) | async-done | bytes 688160 | tf_op jit(solution)/shard_map/all_to_all | solution.py:44
  136.4 5.6 %all-to-all-start.4 = ((bf16[32,1,1]{2,1,0:T(2,128)(2,1)}), bf16[32,1,1]{2,1,0:T(2,128)(2,1)S(1)}, u32[]{:S(2)}, u32[]{:S(2)}) async-start(bf16[32,1,1]{2,1,0:T(2,128)(2,1)} %copy.52), calls=%async_computation.4 | async-start | bytes 32768 | tf_op jit(solution)/shard_map/all_to_all | solution.py:45
  142.3 8.3 %all-to-all-done.4 = bf16[32,1,1]{2,1,0:T(2,128)(2,1)S(1)} async-done(((bf16[32,1,1]{2,1,0:T(2,128)(2,1)}), bf16[32,1,1]{2,1,0:T(2,128)(2,1)S(1)}, u32[]{:S(2)}, u32[]{:S(2)}) %all-to-all-start.4) | async-done | bytes 96 | tf_op jit(solution)/shard_map/all_to_all | solution.py:45
  150.5 5.1 %stack.3 = bf16[16,768,448]{1,2,0:T(8,128)(2,1)} broadcast(bf16[768,448]{0,1:T(8,128)(2,1)S(1)} %copy.48), dimensions={1,2} | broadcast | bytes 11698176 | tf_op jit(solution)/shard_map/stack | solution.py:49
  155.6 5.0 all-to-all-start.1
  161.4 239.6 %all-to-all-done.1 = bf16[16,768,448]{1,2,0:T(8,128)(2,1)} async-done(((bf16[16,768,448]{1,2,0:T(8,128)(2,1)}), bf16[16,768,448]{1,2,0:T(8,128)(2,1)}, u32[]{:S(2)}, u32[]{:S(2)}) %all-to-all-start.1) | async-done | bytes 11010080 | tf_op jit(solution)/shard_map/all_to_all | solution.py:49
  401.0 6.0 %multiply_reduce_fusion = (f32[768]{0:T(1024)S(1)}, f32[768,128]{0,1:T(8,128)S(1)}) fusion(bf16[768,7168]{0,1:T(8,128)(2,1)} %bitcast.7, bf16[1,7168,128]{2,1,0:T(8,128)(2,1)S(1)} %copy-done), kind=kOutput, calls=%fused_computation.14 | convolution fusion | flops 1409481984 | bytes 13241344 | tf_op jit(solution)/shard_map/dot_general | solution.py:51
  407.0 5.9 %fusion.11 = f32[768]{0:T(1024)S(1)} fusion(f32[768,128]{0,1:T(8,128)S(1)} %get-tuple-element.9, bf16[768,7168]{0,1:T(8,128)(2,1)} %bitcast.7, bf16[1,7168,128]{2,1,0:T(8,128)(2,1)S(1)} %copy-done.5), kind=kOutput, calls=%fused_computation.13 | convolution fusion | flops 1409580288 | bytes 13241344 | tf_op jit(solution)/shard_map/dot_general | solution.py:52
  413.1 46.9 %all-reduce = (f32[32,24]{1,0:T(8,128)}, f32[32,24]{1,0:T(8,128)}) all-reduce(f32[32,24]{1,0:T(8,128)S(1)} %div.36, f32[32,24]{1,0:T(8,128)S(1)} %div.34), channel_id=1, replica_groups=mesh['expert'=32,'tensor'=16] {'tensor'}, use_global_device_ids=true, to_apply=%region_10.12 | all-reduce | flops 1536 | bytes 12288 | tf_op jit(solution)/shard_map/psum | solution.py:59
  460.1 4.7 all-to-all-start.2
  465.1 8.4 %all-to-all-done.2 = f32[32,1,24]{2,1,0:T(1,128)S(1)} async-done(((f32[32,1,24]{2,1,0:T(1,128)}), f32[32,1,24]{2,1,0:T(1,128)S(1)}, u32[]{:S(2)}, u32[]{:S(2)}) %all-to-all-start.2) | async-done | bytes 3104 | tf_op jit(solution)/shard_map/all_to_all | solution.py:62
  473.4 5.0 all-to-all-start.3
  478.4 1.2 multiply_divide_fusion
  479.6 1.3 reduce_sum.99
  481.0 1.3 reduce_sum.100
  484.9 2.1 all-to-all-done.3
  487.8 2.3 gather_fusion
  490.1 2.3 gather_fusion.1
  (52 shorter events, 8.0 us)
Async XLA Ops:
  7.2 393.8 %copy-start = (bf16[1,7168,128]{2,1,0:T(8,128)(2,1)S(1)}, bf16[1,7168,128]{2,1,0:T(8,128)(2,1)}, u32[]{:S(2)}) copy-start(bf16[1,7168,128]{2,1,0:T(8,128)(2,1)} %param.14) | copy-start | bytes 5505028
  7.2 70.6 %reduce-scatter.4.cloned.1.call-start = ((), (), s32[]{:S(2)}) async-start(), calls=%async_computation.6 | async-start | bytes 1949696
  7.2 2.8 copy-start.2
  7.2 3.1 copy-start.4
  10.0 68.8 %copy-start.1 = (bf16[64,448]{1,0:T(8,128)(2,1)S(1)}, bf16[64,448]{1,0:T(8,128)(2,1)}, u32[]{:S(2)}) copy-start(bf16[64,448]{1,0:T(8,128)(2,1)} %param.9) | copy-start | bytes 172036
  104.2 32.3 %all-to-all-start = ((bf16[32,24,448]{2,1,0:T(8,128)(2,1)}), bf16[32,24,448]{2,1,0:T(8,128)(2,1)S(1)}, u32[]{:S(2)}, u32[]{:S(2)}) async-start(bf16[32,24,448]{2,1,0:T(8,128)(2,1)} %bitcast.4), calls=%async_computation | async-start | bytes 1572864 | tf_op jit(solution)/shard_map/all_to_all | solution.py:44
  136.4 14.1 %all-to-all-start.4 = ((bf16[32,1,1]{2,1,0:T(2,128)(2,1)}), bf16[32,1,1]{2,1,0:T(2,128)(2,1)S(1)}, u32[]{:S(2)}, u32[]{:S(2)}) async-start(bf16[32,1,1]{2,1,0:T(2,128)(2,1)} %copy.52), calls=%async_computation.4 | async-start | bytes 32768 | tf_op jit(solution)/shard_map/all_to_all | solution.py:45
  155.6 5.0 copy-start.3
  155.6 245.4 %all-to-all-start.1 = ((bf16[16,768,448]{1,2,0:T(8,128)(2,1)}), bf16[16,768,448]{1,2,0:T(8,128)(2,1)}, u32[]{:S(2)}, u32[]{:S(2)}) async-start(bf16[16,768,448]{1,2,0:T(8,128)(2,1)} %stack.3), calls=%async_computation.1 | async-start | bytes 22020096 | tf_op jit(solution)/shard_map/all_to_all | solution.py:49
  401.0 6.0 %copy-start.5 = (bf16[1,7168,128]{2,1,0:T(8,128)(2,1)S(1)}, bf16[1,7168,128]{2,1,0:T(8,128)(2,1)}, u32[]{:S(2)}) copy-start(bf16[1,7168,128]{2,1,0:T(8,128)(2,1)} %param.15) | copy-start | bytes 5505028
  460.1 13.4 %all-to-all-start.2 = ((f32[32,1,24]{2,1,0:T(1,128)}), f32[32,1,24]{2,1,0:T(1,128)S(1)}, u32[]{:S(2)}, u32[]{:S(2)}) async-start(f32[32,1,24]{2,1,0:T(1,128)} %bitcast.12), calls=%async_computation.2 | async-start | bytes 32768 | tf_op jit(solution)/shard_map/all_to_all | solution.py:62
  473.4 13.6 %all-to-all-start.3 = ((f32[32,1,24]{2,1,0:T(1,128)}), f32[32,1,24]{2,1,0:T(1,128)S(1)}, u32[]{:S(2)}, u32[]{:S(2)}) async-start(f32[32,1,24]{2,1,0:T(1,128)} %bitcast.14), calls=%async_computation.3 | async-start | bytes 32768 | tf_op jit(solution)/shard_map/all_to_all | solution.py:63
Sparse Core Ops, SparseCore 0:
  10.9 66.8 reduce-scatter.3
